TPU v7x, 128 devices: a whole 4x4x4 slice. The times are simulated.
128 devices in a mesh: row: 16 (over y, x), col: 8 (over z, core).
Axes of the slice: x: 4, y: 4, z: 4, core: 2. Of those that a mesh axis runs over, the one named last changes fastest.
Arguments:
- orbitals: float32 [32768, 1024], P('row', 'col'), may hold values from -6 to 6
- point_index: int32 [8192], replicated, may hold values from 0 to 32767, as said below
- coulomb: float32 [8192, 8192], P('row', 'col'), may hold values from -0.001953125 to 0.001953125
- fitting: float32 [32768, 8192], P('row', 'col'), may hold values from -0.0625 to 0.0625
Outputs:
- exchange_out: float32 [32768, 1024], P('row', 'col')
Inputs may be any that keep to these rules, and one draw needn't show every extreme that they name: `point_index`: indices are distinct. Grid index g lies in slab g // 2048. Of the 512 consecutive points of each row panel, at most 64 lie in one slab, and in every panel exactly 64 lie in one slab.
All inputs are finite; a program needn't handle non-finite values.
Results may differ from a plain program's by a relative error of at most 0.00012.
Values sent between devices are 32-bit elements; how exact they have to be, the bound alone decides.
No kernel may reach another device: no remote copies, remote signals or barrier semaphores. Data moves between devices by JAX's collectives and lax.ppermute only.
A program may use at most 64 MiB of HBM per device.

v0:
```python
import jax
import jax.numpy as jnp
from jax import lax
from jax.sharding import PartitionSpec as P


def per_device(orbitals, point_index, coulomb, fitting):
    row_count = lax.axis_size("row")
    slab_rows = orbitals.shape[0]
    band_cols = orbitals.shape[1]
    total_points = point_index.shape[0]
    per_panel = total_points // row_count
    slot_count = 2 * per_panel // row_count
    my_row = lax.axis_index("row")
    my_col = lax.axis_index("col")
    owner = point_index // slab_rows
    local_row = point_index - owner * slab_rows
    owner_grid = owner.reshape(row_count, per_panel)
    local_grid = local_row.reshape(row_count, per_panel)
    matches = (owner_grid[:, :, None] == jnp.arange(row_count)[None, None, :]).astype(jnp.int32)
    ranking = jnp.cumsum(matches, axis=1) - 1
    slot_grid = jnp.sum(jnp.where(matches > 0, ranking, 0), axis=2)
    mine = owner_grid == my_row
    chosen = mine[:, :, None] & (slot_grid[:, :, None] == jnp.arange(slot_count)[None, None, :])
    source_row = jnp.sum(jnp.where(chosen, local_grid[:, :, None], 0), axis=1)
    valid = jnp.any(chosen, axis=1)
    outgoing = jnp.where(valid[:, :, None], orbitals[source_row], 0.0)
    received = lax.all_to_all(outgoing, "row", split_axis=0, concat_axis=0, tiled=True)
    flattened = received.reshape(row_count * slot_count, band_cols)
    owner_mine = lax.dynamic_slice_in_dim(owner_grid, my_row, 1, 0)[0]
    slot_mine = lax.dynamic_slice_in_dim(slot_grid, my_row, 1, 0)[0]
    panel_strip = flattened[owner_mine * slot_count + slot_mine]
    panel_full = lax.all_gather(panel_strip, "col", axis=1, tiled=True)
    strip_all = lax.all_gather(panel_strip, "row", axis=0, tiled=True)
    column_full = lax.all_to_all(strip_all, "col", split_axis=0, concat_axis=1, tiled=True)
    pair = jnp.dot(
        panel_full,
        column_full.T,
        precision=lax.Precision.HIGHEST,
        preferred_element_type=jnp.float32,
    )
    partial_value = jnp.dot(
        coulomb * pair,
        column_full,
        precision=lax.Precision.HIGHEST,
        preferred_element_type=jnp.float32,
    )
    summed = lax.psum(partial_value, "col")
    weight_strip = lax.dynamic_slice_in_dim(summed, my_col * band_cols, band_cols, 1)
    weight_all = lax.all_gather(weight_strip, "row", axis=0, tiled=True)
    weight_column = lax.all_to_all(weight_all, "col", split_axis=0, concat_axis=1, tiled=True)
    term = -jnp.dot(
        fitting, weight_column, precision=lax.Precision.HIGHEST, preferred_element_type=jnp.float32
    )
    return lax.psum_scatter(term, "col", scatter_dimension=1, tiled=True)


def solution(mesh):
    in_specs = (P("row", "col"), P(), P("row", "col"), P("row", "col"))
    out_specs = P("row", "col")
    return jax.shard_map(
        per_device, mesh=mesh, in_specs=in_specs, out_specs=out_specs, check_vma=False
    )
```

profile of v0, /device:TPU:1, one launch (start us, length us, event | category | flops | bytes accessed | tf_op | source)
XLA Modules:
  0.0 455.0 jit_solution(17053227646644260959)
XLA Ops:
  6.5 0.0 copy-start
  6.5 0.9 add_select_fusion
  7.4 0.1 fusion.6
  7.5 18.1 %reduce-window.6 = s32[16,16,4,128]{3,1,2,0:T(8,128)S(1)} reduce-window(s32[16,16,4,128]{3,1,2,0:T(8,128)S(1)} %fusion.6, s32[]{:T(128)} %constant.16.clone.1), window={size=1x1x1x128 pad=0_0x0_0x0_0x127_0}, to_apply=%region_0.1 | reduce-window | flops 16646144 | bytes 1048580 | tf_op jit(solution)/shard_map/reduce-window
  25.6 0.2 slice.12
  25.9 0.4 copy.12
  26.3 0.1 fusion.8
  26.5 0.2 fusion.5
  26.7 0.4 fusion.3
  27.1 0.5 select_reduce_fusion
  27.7 0.1 reshape.84
  27.7 0.0 copy-done
  27.7 2.8 gather_fusion
  30.6 1.0 broadcast_select_fusion
  31.6 7.6 %all-to-all-start = ((f32[16,64,128]{2,1,0:T(8,128)}), f32[16,64,128]{2,1,0:T(8,128)S(1)}, u32[]{:S(2)}, u32[]{:S(2)}) async-start(f32[16,64,128]{2,1,0:T(8,128)} %broadcast_select_fusion), calls=%async_computation | async-start | bytes 1048576 | tf_op jit(solution)/shard_map/all_to_all | solution.py:28
  39.1 0.0 all-gather.10.cloned.1.call-start
  39.2 10.3 %all-to-all-done = f32[16,64,128]{2,1,0:T(8,128)S(1)} async-done(((f32[16,64,128]{2,1,0:T(8,128)}), f32[16,64,128]{2,1,0:T(8,128)S(1)}, u32[]{:S(2)}, u32[]{:S(2)}) %all-to-all-start) | async-done | bytes 524320 | tf_op jit(solution)/shard_map/all_to_all | solution.py:28
  49.6 1.6 gather_fusion.1
  51.2 0.0 all-gather.10.cloned.1.call-update
  51.2 0.0 all-gather.8.cloned.1.call-start
  51.3 0.7 all-gather.8.cloned.1.call-update
  52.0 50.4 %all-gather.10.cloned.1.call-done = f32[8192,128]{1,0:T(8,128)} async-done(((f32[512,128]{1,0:T(8,128)}), f32[8192,128]{1,0:T(8,128)}) %all-gather.10.cloned.1.call-update) | async-done | bytes 4194320 | tf_op jit(solution)/shard_map/all_gather | solution.py:34
  102.4 5.4 %copy.15 = f32[8,1024,128]{1,2,0:T(8,128)} copy(f32[8,1024,128]{2,1,0:T(8,128)} %bitcast.44) | data formatting | bytes 8388608 | tf_op jit(solution)/shard_map/all_to_all | solution.py:35
  107.7 5.3 %all-to-all-start.1 = ((f32[8,1024,128]{1,2,0:T(8,128)}), f32[8,1024,128]{1,2,0:T(8,128)}, u32[]{:S(2)}, u32[]{:S(2)}) async-start(f32[8,1024,128]{1,2,0:T(8,128)} %copy.15), calls=%async_computation.1 | async-start | bytes 8388608 | tf_op jit(solution)/shard_map/all_to_all | solution.py:35
  113.0 0.0 all-reduce.2.cloned.1.call-start
  113.0 31.5 %all-gather.8.cloned.1.call-done = f32[512,1024]{1,0:T(8,128)} async-done(((f32[512,128]{1,0:T(8,128)}), f32[512,1024]{1,0:T(8,128)}) %all-gather.8.cloned.1.call-update) | async-done | bytes 2097168 | tf_op jit(solution)/shard_map/all_gather | solution.py:33
  144.5 25.7 %all-to-all-done.1 = f32[8,1024,128]{1,2,0:T(8,128)} async-done(((f32[8,1024,128]{1,2,0:T(8,128)}), f32[8,1024,128]{1,2,0:T(8,128)}, u32[]{:S(2)}, u32[]{:S(2)}) %all-to-all-start.1) | async-done | bytes 4194336 | tf_op jit(solution)/shard_map/all_to_all | solution.py:35
  170.2 0.0 copy-start.1
  170.2 9.8 %fusion.11 = f32[512,1024]{1,0:T(8,128)S(1)} fusion(f32[512,1024]{1,0:T(8,128)} %all-gather.8.cloned.1.call-done, f32[1024,1024]{0,1:T(8,128)} %bitcast.10), kind=kOutput, calls=%fused_computation.34 | convolution fusion | flops 6442450944 | bytes 8388608 | tf_op jit(solution)/shard_map/dot_general | solution.py:36
  180.0 0.0 copy-done.1
  180.0 9.8 %fusion = f32[512,1024]{1,0:T(8,128)} fusion(f32[1024,1024]{0,1:T(8,128)} %bitcast.10, f32[512,1024]{1,0:T(8,128)S(1)} %copy-done.1, f32[512,1024]{1,0:T(8,128)S(1)} %fusion.11), kind=kOutput, calls=%fused_computation.3 | convolution fusion | flops 6442975232 | bytes 10485760 | tf_op jit(solution)/shard_map/dot_general | solution.py:42
  189.8 0.0 all-reduce.2.cloned.1.call-update
  189.8 0.0 all-gather.6.cloned.1.call-start
  189.9 62.2 %all-reduce.2.cloned.1.call-done = f32[512,1024]{1,0:T(8,128)} async-done(((f32[512,1024]{1,0:T(8,128)}), f32[512,1024]{1,0:T(8,128)}) %all-reduce.2.cloned.1.call-update) | async-done | bytes 2097168 | tf_op jit(solution)/shard_map/psum | solution.py:48
  252.1 1.7 constant_dynamic-slice_fusion
  253.7 0.0 all-gather.6.cloned.1.call-update
  253.7 0.0 reduce-scatter.2.cloned.1.call-start
  253.8 52.7 %all-gather.6.cloned.1.call-done = f32[8192,128]{1,0:T(8,128)} async-done(((f32[512,128]{1,0:T(8,128)}), f32[8192,128]{1,0:T(8,128)}) %all-gather.6.cloned.1.call-update) | async-done | bytes 4194320 | tf_op jit(solution)/shard_map/all_gather | solution.py:50
  306.5 5.4 %copy.16 = f32[8,1024,128]{1,2,0:T(8,128)} copy(f32[8,1024,128]{2,1,0:T(8,128)} %bitcast.45) | data formatting | bytes 8388608 | tf_op jit(solution)/shard_map/all_to_all | solution.py:51
  311.9 53.9 %all_to_all.43 = f32[8,1024,128]{1,2,0:T(8,128)S(1)} all-to-all(f32[8,1024,128]{1,2,0:T(8,128)} %copy.16), channel_id=1, replica_groups=mesh['row'=16,'col'=8] {'col'}, dimensions={0} | all-to-all | bytes 8388608 | tf_op jit(solution)/shard_map/all_to_all | solution.py:51
  365.8 29.9 %negate_bitcast_fusion = f32[2048,1024]{0,1:T(8,128)} fusion(f32[1024,1024]{0,1:T(8,128)S(1)} %bitcast.46, f32[2048,1024]{1,0:T(8,128)} %param.7), kind=kOutput, calls=%fused_computation.2 | convolution fusion | flops 25771900928 | bytes 20971520 | tf_op jit(solution)/shard_map/dot_general | solution.py:52
  395.6 0.0 reduce-scatter.2.cloned.1.call-update
  395.7 50.2 %reduce-scatter.2.cloned.1.call-done = f32[2048,128]{0,1:T(8,128)} async-done(((f32[2048,1024]{0,1:T(8,128)}), f32[2048,128]{0,1:T(8,128)}) %reduce-scatter.2.cloned.1.call-update) | async-done | bytes 1048592 | tf_op jit(solution)/shard_map/reduce_scatter | solution.py:55
  445.9 2.5 copy.17
  (9 shorter events, 0.1 us)
Async XLA Ops:
  6.5 21.2 %copy-start = (f32[2048,128]{1,0:T(8,128)S(1)}, f32[2048,128]{1,0:T(8,128)}, u32[]{:S(2)}) copy-start(f32[2048,128]{1,0:T(8,128)} %param.4) | copy-start | bytes 3145732
  31.6 18.0 %all-to-all-start = ((f32[16,64,128]{2,1,0:T(8,128)}), f32[16,64,128]{2,1,0:T(8,128)S(1)}, u32[]{:S(2)}, u32[]{:S(2)}) async-start(f32[16,64,128]{2,1,0:T(8,128)} %broadcast_select_fusion), calls=%async_computation | async-start | bytes 1048576 | tf_op jit(solution)/shard_map/all_to_all | solution.py:28
  39.1 63.2 %all-gather.10.cloned.1.call-start = ((), (), s32[]{:S(2)}) async-start(), calls=%async_computation.8 | async-start | bytes 4456448 | tf_op jit(solution)/shard_map/all_gather | solution.py:34
  51.2 93.3 %all-gather.8.cloned.1.call-start = ((), (), s32[]{:S(2)}) async-start(), calls=%async_computation.7 | async-start | bytes 2359296 | tf_op jit(solution)/shard_map/all_gather | solution.py:33
  107.7 62.5 %all-to-all-start.1 = ((f32[8,1024,128]{1,2,0:T(8,128)}), f32[8,1024,128]{1,2,0:T(8,128)}, u32[]{:S(2)}, u32[]{:S(2)}) async-start(f32[8,1024,128]{1,2,0:T(8,128)} %copy.15), calls=%async_computation.1 | async-start | bytes 8388608 | tf_op jit(solution)/shard_map/all_to_all | solution.py:35
  113.0 139.1 %all-reduce.2.cloned.1.call-start = ((), (), s32[]{:S(2)}) async-start(), calls=%async_computation.4 | async-start | bytes 4194304 | tf_op jit(solution)/shard_map/psum | solution.py:48
  170.2 9.8 %copy-start.1 = (f32[512,1024]{1,0:T(8,128)S(1)}, f32[512,1024]{1,0:T(8,128)}, u32[]{:S(2)}) copy-start(f32[512,1024]{1,0:T(8,128)} %param.6) | copy-start | bytes 6291460
  189.8 116.7 %all-gather.6.cloned.1.call-start = ((), (), s32[]{:S(2)}) async-start(), calls=%async_computation.5 | async-start | bytes 4456448 | tf_op jit(solution)/shard_map/all_gather | solution.py:50
  253.7 192.2 %reduce-scatter.2.cloned.1.call-start = ((), (), s32[]{:S(2)}) async-start(), calls=%async_computation.6 | async-start | bytes 9437184 | tf_op jit(solution)/shard_map/reduce_scatter | solution.py:55
Sparse Core Ops, SparseCore 0:
  51.3 50.9 all-gather.9
  104.0 40.3 all-gather.7
  190.0 62.0 all-reduce.1
  254.1 52.4 all-gather.5
  395.8 50.0 reduce-scatter.1
where the time goes:
time: 456 us; the launch traced here: 455 us
  waiting for transfers between devices  284 us (62%)
  blocking collectives  53.9 us (12%)
  matrix products  49.4 us (11%)
  other arithmetic  21.4 us (5%)
  local copies, waits for them, and re-layouts  20.1 us (4%)
  between operations  13.3 us (3%)
  starting transfers between devices  13 us (3%)
    psum x1, waiting for transfers between devices, per_device(): summed = lax.psum(partial_value, 'col')  62.2 us
    all_to_all x1, blocking collectives, per_device(): lax.all_to_all(weight_all, 'col', split_axis=0, concat_axis=1, tiled=True)  53.9 us
    all_gather x1, waiting for transfers between devices, per_device(): weight_all = lax.all_gather(weight_strip, 'row', axis=0, tiled=True)  52.7 us
    all_gather x1, waiting for transfers between devices, per_device(): strip_all = lax.all_gather(panel_strip, 'row', axis=0, tiled=True)  50.4 us
    reduce_scatter x1, waiting for transfers between devices, per_device(): return lax.psum_scatter(term, 'col', scatter_dimension=1, tiled=True)  50.2 us
    all_gather x1, waiting for transfers between devices, per_device(): panel_full = lax.all_gather(panel_strip, 'col', axis=1, tiled=True)  31.5 us
    dot_general x1, matrix products, per_device(): jnp.dot(fitting, weight_column, precision=lax.Precision.HIGHEST, preferre...  29.9 us
    all_to_all x1, waiting for transfers between devices, per_device(): lax.all_to_all(strip_all, 'col', split_axis=0, concat_axis=1, tiled=True)  25.7 us
  transfers between devices with their start and end apart: 7, of which 7 were waited for; matrix products, arithmetic and copies ran while one was open for 1% of the time, Pallas kernels for 0%

commit v1 on v0

--- a/solution.py
+++ b/solution.py
@@ -31,7 +31,9 @@
     slot_mine = lax.dynamic_slice_in_dim(slot_grid, my_row, 1, 0)[0]
     panel_strip = flattened[owner_mine * slot_count + slot_mine]
     panel_full = lax.all_gather(panel_strip, "col", axis=1, tiled=True)
-    strip_all = lax.all_gather(panel_strip, "row", axis=0, tiled=True)
+    strip_all = jnp.concatenate(
+        lax.all_to_all(jnp.stack([panel_strip] * lax.axis_size("row")), "row", 0, 0), axis=0
+    )
     column_full = lax.all_to_all(strip_all, "col", split_axis=0, concat_axis=1, tiled=True)
     pair = jnp.dot(
         panel_full,

time: 456 us -> 457 us (level)
  waiting for transfers between devices: 284 us -> 230 us
  blocking collectives: 53.9 us -> 107 us
    all_to_all x0 -> x1, blocking collectives: none -> 53.2 us  [per_device(): lax.all_to_all(jnp.stack([panel_strip] * lax.axis_size('row')), 'row', 0, 0)]
    all_gather x1 -> x0, waiting for transfers between devices: 50.4 us -> none  [per_device(): strip_all = lax.all_gather(panel_strip, 'row', axis=0, tiled=True)]
    all_gather x1, waiting for transfers between devices: 31.5 us -> 0.01 us  [per_device(): panel_full = lax.all_gather(panel_strip, 'col', axis=1, tiled=True)]
    all_to_all x1, waiting for transfers between devices: 25.7 us -> 56.3 us  [per_device(): lax.all_to_all(strip_all, 'col', split_axis=0, concat_axis=1, tiled=True)]
  transfers between devices with their start and end apart: 7 -> 6, of which waited for: 7 -> 5; matrix products, arithmetic and copies ran while one was open for 1% -> 1% of each run, Pallas kernels for 0% -> 0%
where the time goes in v1:
time: 457 us; the launch traced here: 456 us
  waiting for transfers between devices  230 us (50%)
  blocking collectives  107 us (23%)
  matrix products  47.9 us (10%)
  other arithmetic  21.4 us (5%)
  local copies, waits for them, and re-layouts  20.2 us (4%)
  starting transfers between devices  15.9 us (3%)
  between operations  13.3 us (3%)
    psum x1, waiting for transfers between devices, per_device(): summed = lax.psum(partial_value, 'col')  59.7 us
    all_to_all x1, waiting for transfers between devices, per_device(): lax.all_to_all(strip_all, 'col', split_axis=0, concat_axis=1, tiled=True)  56.3 us
    all_to_all x1, blocking collectives, per_device(): lax.all_to_all(weight_all, 'col', split_axis=0, concat_axis=1, tiled=True)  53.9 us
    all_to_all x1, blocking collectives, per_device(): lax.all_to_all(jnp.stack([panel_strip] * lax.axis_size('row')), 'row', 0, 0)  53.2 us
    all_gather x1, waiting for transfers between devices, per_device(): weight_all = lax.all_gather(weight_strip, 'row', axis=0, tiled=True)  52.9 us
    reduce_scatter x1, waiting for transfers between devices, per_device(): return lax.psum_scatter(term, 'col', scatter_dimension=1, tiled=True)  50.2 us
    dot_general x1, matrix products, per_device(): jnp.dot(fitting, weight_column, precision=lax.Precision.HIGHEST, preferre...  29.9 us
    another operation x2, other arithmetic  18.3 us
  transfers between devices with their start and end apart: 6, of which 5 were waited for; matrix products, arithmetic and copies ran while one was open for 1% of the time, Pallas kernels for 0%

profile of v1, /device:TPU:1, one launch (start us, length us, event | category | flops | bytes accessed | tf_op | source)
XLA Modules:
  0.0 456.0 jit_solution(13357987782297757439)
XLA Ops:
  6.5 0.0 copy-start
  6.5 0.9 add_select_fusion
  7.4 0.1 fusion.6
  7.5 18.1 %reduce-window.6 = s32[16,16,4,128]{3,1,2,0:T(8,128)S(1)} reduce-window(s32[16,16,4,128]{3,1,2,0:T(8,128)S(1)} %fusion.6, s32[]{:T(128)} %constant.16.clone.1), window={size=1x1x1x128 pad=0_0x0_0x0_0x127_0}, to_apply=%region_0.1 | reduce-window | flops 16646144 | bytes 1048580 | tf_op jit(solution)/shard_map/reduce-window
  25.6 0.2 slice.12
  25.9 0.4 copy.17
  26.3 0.1 fusion.8
  26.5 0.2 fusion.5
  26.7 0.4 fusion.3
  27.1 0.5 select_reduce_fusion
  27.7 0.1 reshape.88
  27.7 0.0 copy-done
  27.7 2.8 gather_fusion
  30.6 1.0 broadcast_select_fusion
  31.6 7.6 %all-to-all-start = ((f32[16,64,128]{2,1,0:T(8,128)}), f32[16,64,128]{2,1,0:T(8,128)S(1)}, u32[]{:S(2)}, u32[]{:S(2)}) async-start(f32[16,64,128]{2,1,0:T(8,128)} %broadcast_select_fusion), calls=%async_computation | async-start | bytes 1048576 | tf_op jit(solution)/shard_map/all_to_all | solution.py:28
  39.2 10.4 %all-to-all-done = f32[16,64,128]{2,1,0:T(8,128)S(1)} async-done(((f32[16,64,128]{2,1,0:T(8,128)}), f32[16,64,128]{2,1,0:T(8,128)S(1)}, u32[]{:S(2)}, u32[]{:S(2)}) %all-to-all-start) | async-done | bytes 524320 | tf_op jit(solution)/shard_map/all_to_all | solution.py:28
  49.6 1.0 gather_fusion.1
  50.6 0.0 copy-start.2
  50.6 0.4 stack.2
  51.0 0.3 copy-done.2
  51.3 53.2 %all_to_all.48 = f32[16,512,128]{2,1,0:T(8,128)} all-to-all(f32[16,512,128]{2,1,0:T(8,128)S(1)} %stack.2), channel_id=1, replica_groups=mesh['row'=16,'col'=8] {'row'}, dimensions={0} | all-to-all | bytes 8388608 | tf_op jit(solution)/shard_map/all_to_all | solution.py:35
  104.5 8.0 %all-to-all-start.2 = ((f32[8,1024,128]{2,1,0:T(8,128)}), f32[8,1024,128]{2,1,0:T(8,128)}, u32[]{:S(2)}, u32[]{:S(2)}) async-start(f32[8,1024,128]{2,1,0:T(8,128)} %bitcast.44), calls=%async_computation.2 | async-start | bytes 8388608 | tf_op jit(solution)/shard_map/all_to_all | solution.py:37
  112.5 0.0 all-gather.6.cloned.1.call-start
  112.5 0.7 all-gather.6.cloned.1.call-update
  113.2 0.2 all-reduce.2.cloned.1.call-start
  113.5 56.3 %all-to-all-done.2 = f32[8,1024,128]{2,1,0:T(8,128)} async-done(((f32[8,1024,128]{2,1,0:T(8,128)}), f32[8,1024,128]{2,1,0:T(8,128)}, u32[]{:S(2)}, u32[]{:S(2)}) %all-to-all-start.2) | async-done | bytes 4194336 | tf_op jit(solution)/shard_map/all_to_all | solution.py:37
  169.7 5.4 %copy.20 = f32[1024,8,128]{0,2,1:T(8,128)} copy(f32[1024,8,128]{2,0,1:T(8,128)} %bitcast.9) | data formatting | bytes 8388608 | tf_op jit(solution)/shard_map/all_to_all | solution.py:37
  175.1 0.0 all-gather.6.cloned.1.call-done
  175.1 0.0 copy-start.1
  175.1 0.0 copy-start.3
  175.1 9.8 %fusion.11 = f32[512,1024]{1,0:T(8,128)S(1)} fusion(f32[512,1024]{1,0:T(8,128)} %all-gather.6.cloned.1.call-done, f32[1024,1024]{0,1:T(8,128)} %bitcast.42), kind=kOutput, calls=%fused_computation.34 | convolution fusion | flops 6442450944 | bytes 8388608 | tf_op jit(solution)/shard_map/dot_general | solution.py:38
  184.9 0.0 copy-done.1
  184.9 0.0 copy-done.3
  184.9 8.2 %fusion = f32[512,1024]{1,0:T(8,128)} fusion(f32[1024,1024]{0,1:T(8,128)S(1)} %bitcast.43, f32[512,1024]{1,0:T(8,128)S(1)} %copy-done.3, f32[512,1024]{1,0:T(8,128)S(1)} %fusion.11), kind=kOutput, calls=%fused_computation.3 | convolution fusion | flops 6442975232 | bytes 10485760 | tf_op jit(solution)/shard_map/dot_general | solution.py:44
  193.1 0.0 all-reduce.2.cloned.1.call-update
  193.2 0.0 all-gather.4.cloned.1.call-start
  193.2 59.7 %all-reduce.2.cloned.1.call-done = f32[512,1024]{1,0:T(8,128)} async-done(((f32[512,1024]{1,0:T(8,128)}), f32[512,1024]{1,0:T(8,128)}) %all-reduce.2.cloned.1.call-update) | async-done | bytes 2097168 | tf_op jit(solution)/shard_map/psum | solution.py:50
  252.9 1.7 constant_dynamic-slice_fusion
  254.6 0.0 all-gather.4.cloned.1.call-update
  254.6 0.0 reduce-scatter.2.cloned.1.call-start
  254.7 52.9 %all-gather.4.cloned.1.call-done = f32[8192,128]{1,0:T(8,128)} async-done(((f32[512,128]{1,0:T(8,128)}), f32[8192,128]{1,0:T(8,128)}) %all-gather.4.cloned.1.call-update) | async-done | bytes 4194320 | tf_op jit(solution)/shard_map/all_gather | solution.py:52
  307.6 5.4 %copy.21 = f32[8,1024,128]{1,2,0:T(8,128)} copy(f32[8,1024,128]{2,1,0:T(8,128)} %bitcast.46) | data formatting | bytes 8388608 | tf_op jit(solution)/shard_map/all_to_all | solution.py:53
  312.9 53.9 %all_to_all.49 = f32[8,1024,128]{1,2,0:T(8,128)S(1)} all-to-all(f32[8,1024,128]{1,2,0:T(8,128)} %copy.21), channel_id=1, replica_groups=mesh['row'=16,'col'=8] {'col'}, dimensions={0} | all-to-all | bytes 8388608 | tf_op jit(solution)/shard_map/all_to_all | solution.py:53
  366.8 29.9 %negate_bitcast_fusion = f32[2048,1024]{0,1:T(8,128)} fusion(f32[1024,1024]{0,1:T(8,128)S(1)} %bitcast.47, f32[2048,1024]{1,0:T(8,128)} %param.7), kind=kOutput, calls=%fused_computation.2 | convolution fusion | flops 25771900928 | bytes 20971520 | tf_op jit(solution)/shard_map/dot_general | solution.py:54
  396.7 0.0 reduce-scatter.2.cloned.1.call-update
  396.7 50.2 %reduce-scatter.2.cloned.1.call-done = f32[2048,128]{0,1:T(8,128)} async-done(((f32[2048,1024]{0,1:T(8,128)}), f32[2048,128]{0,1:T(8,128)}) %reduce-scatter.2.cloned.1.call-update) | async-done | bytes 1048592 | tf_op jit(solution)/shard_map/reduce_scatter | solution.py:57
  446.9 2.5 copy.22
  (9 shorter events, 0.1 us)
Async XLA Ops:
  6.5 21.2 %copy-start = (f32[2048,128]{1,0:T(8,128)S(1)}, f32[2048,128]{1,0:T(8,128)}, u32[]{:S(2)}) copy-start(f32[2048,128]{1,0:T(8,128)} %param.4) | copy-start | bytes 3145732
  31.6 18.0 %all-to-all-start = ((f32[16,64,128]{2,1,0:T(8,128)}), f32[16,64,128]{2,1,0:T(8,128)S(1)}, u32[]{:S(2)}, u32[]{:S(2)}) async-start(f32[16,64,128]{2,1,0:T(8,128)} %broadcast_select_fusion), calls=%async_computation | async-start | bytes 1048576 | tf_op jit(solution)/shard_map/all_to_all | solution.py:28
  50.6 0.7 copy-start.2
  104.5 65.2 %all-to-all-start.2 = ((f32[8,1024,128]{2,1,0:T(8,128)}), f32[8,1024,128]{2,1,0:T(8,128)}, u32[]{:S(2)}, u32[]{:S(2)}) async-start(f32[8,1024,128]{2,1,0:T(8,128)} %bitcast.44), calls=%async_computation.2 | async-start | bytes 8388608 | tf_op jit(solution)/shard_map/all_to_all | solution.py:37
  112.5 62.6 %all-gather.6.cloned.1.call-start = ((), (), s32[]{:S(2)}) async-start(), calls=%async_computation.8 | async-start | bytes 2359296 | tf_op jit(solution)/shard_map/all_gather | solution.py:33
  113.2 139.7 %all-reduce.2.cloned.1.call-start = ((), (), s32[]{:S(2)}) async-start(), calls=%async_computation.5 | async-start | bytes 4194304 | tf_op jit(solution)/shard_map/psum | solution.py:50
  175.1 9.8 %copy-start.1 = (f32[1024,8,128]{0,2,1:T(8,128)S(1)}, f32[1024,8,128]{0,2,1:T(8,128)}, u32[]{:S(2)}) copy-start(f32[1024,8,128]{0,2,1:T(8,128)} %copy.20) | copy-start | bytes 12582916
  175.1 9.8 %copy-start.3 = (f32[512,1024]{1,0:T(8,128)S(1)}, f32[512,1024]{1,0:T(8,128)}, u32[]{:S(2)}) copy-start(f32[512,1024]{1,0:T(8,128)} %param.6) | copy-start | bytes 6291460
  193.2 114.4 %all-gather.4.cloned.1.call-start = ((), (), s32[]{:S(2)}) async-start(), calls=%async_computation.6 | async-start | bytes 4456448 | tf_op jit(solution)/shard_map/all_gather | solution.py:52
  254.6 192.3 %reduce-scatter.2.cloned.1.call-start = ((), (), s32[]{:S(2)}) async-start(), calls=%async_computation.7 | async-start | bytes 9437184 | tf_op jit(solution)/shard_map/reduce_scatter | solution.py:57
Sparse Core Ops, SparseCore 0:
  115.0 35.2 all-gather.5
  193.3 59.5 all-reduce.1
  255.1 52.4 all-gather.3
  396.8 50.0 reduce-scatter.1
